TPU v7x, 32 devices: a whole 2x2x4 slice. The times are simulated.
32 devices in a mesh: row: 2 (over x), col: 4 (over z), box: 4 (over y, core).
Axes of the slice: x: 2, y: 2, z: 4, core: 2. Of those that a mesh axis runs over, the one named last changes fastest.
Arguments:
- coeffs: bfloat16 [81920, 512], P(('row', 'box'), 'col'), may hold values from -6 to 6
- reflectors: bfloat16 [81920, 256], P(('row', 'box')), may hold values from -0.078125 to 0.078125
- factor: float32 [256, 256], replicated, may hold values from -0.375 to 0.375
- func_exp: float32 [81920], replicated, may hold values from 0.5 to 20
- func_atom: int32 [81920], replicated, may hold values from 0 to 8191, never falling along the last dimension, each value on 1 to 20 neighbouring positions
- atom_pos: float32 [3, 8192], replicated, may hold values from 0 to 1
- point_pos: float32 [3, 128, 128], P(None, ('row', 'col', 'box')), may hold values from 0 to 1
- send_tiles: int32 [8, 8, 2], replicated, may hold values from 0 to 79, as said below
- box_tiles: int32 [128, 16], P(('row', 'col', 'box')), may hold values from 0 to 15, as said below
- box_count: int32 [128], P(('row', 'col', 'box')), may hold values from 1 to 16
Outputs:
- rotated: bfloat16 [81920, 512], P(('row', 'box'), 'col')
- density: float32 [128, 128], P(('row', 'col', 'box'))
Inputs may be any that keep to these rules, and one draw needn't show every extreme that they name: `send_tiles`: for each basis group and box group the 2 tiles are different local tiles of the basis group. `box_tiles`: the 16 slots listed by a box are different. `func_atom`: never falls along the basis functions; every atom carries 1 to 20 functions.
All inputs are finite; a program needn't handle non-finite values.
Results may differ from a plain program's by a relative error of at most 0.015.
Values may be sent and summed in bfloat16 or wider, within the bound.
A program may use at most 128 MiB of HBM per device.

v0:
```python
import math
import jax
import jax.numpy as jnp
from jax import lax
from jax.sharding import PartitionSpec as P

K = 512
TILE = 128


def box_density(arrived, slot_alpha, slot_centre, listed, count, points):
    alpha = slot_alpha[listed]
    centre = slot_centre[:, listed]
    first = points[0][:, None, None] - centre[0][None]
    dist = first * first
    second = points[1][:, None, None] - centre[1][None]
    dist = dist + second * second
    third = points[2][:, None, None] - centre[2][None]
    dist = dist + third * third
    live = jnp.arange(listed.shape[0], dtype=jnp.int32) < count
    phi = jnp.where(live[None, :, None], jnp.exp(-alpha[None] * dist), 0.0).astype(jnp.bfloat16)
    phi = phi.reshape(points.shape[1], -1)
    block = arrived[listed].reshape(-1, arrived.shape[2])
    orbital = jnp.dot(phi, block, preferred_element_type=jnp.float32)
    return jnp.sum(orbital * orbital, 1) / (K * TILE)


def by_blocks(arrived, slot_alpha, slot_centre, lists, counts, points):
    boxes = lists.shape[0]
    width = math.gcd(boxes, 2)
    steps = boxes // width
    lists_blocked = lists.reshape(steps, width, lists.shape[1])
    counts_blocked = counts.reshape(steps, width)
    moved = jnp.moveaxis(points, 1, 0)
    points_blocked = moved.reshape(steps, width, moved.shape[1], moved.shape[2])
    single = jax.vmap(
        lambda listed, count, where: box_density(
            arrived, slot_alpha, slot_centre, listed, count, where
        )
    )

    def one_block(items):
        return single(items[0], items[1], items[2])

    result = lax.map(one_block, (lists_blocked, counts_blocked, points_blocked))
    return result.reshape(boxes, result.shape[2])


def per_device(
    coeffs,
    reflectors,
    factor,
    func_exp,
    func_atom,
    atom_pos,
    point_pos,
    send_tiles,
    box_tiles,
    box_count,
):
    panel_part = jnp.dot(reflectors.T, coeffs, preferred_element_type=jnp.float32)
    panel = lax.psum(panel_part.astype(jnp.bfloat16), ("row", "box")).astype(jnp.float32)
    scaled = jnp.dot(factor, panel, precision=lax.Precision.HIGHEST).astype(jnp.bfloat16)
    rotated = (
        coeffs.astype(jnp.float32) - jnp.dot(reflectors, scaled, preferred_element_type=jnp.float32)
    ).astype(jnp.bfloat16)
    peers = lax.axis_size(("row", "box"))
    group = lax.axis_index(("row", "box"))
    capacity = send_tiles.shape[2]
    local_tiles = coeffs.shape[0] // TILE
    slots = jnp.arange(peers * capacity, dtype=jnp.int32)
    source = slots // capacity
    within = slots % capacity
    tile = source * local_tiles + send_tiles[source, group, within]
    funcs = tile[:, None] * TILE + jnp.arange(TILE, dtype=jnp.int32)[None, :]
    slot_alpha = func_exp[funcs]
    slot_centre = atom_pos[:, func_atom[funcs]]
    outgoing_index = send_tiles[group]
    outgoing = rotated.reshape(local_tiles, TILE, rotated.shape[1])[outgoing_index]
    arrived = lax.all_to_all(outgoing, ("row", "box"), split_axis=0, concat_axis=0, tiled=True)
    arrived = arrived.reshape(peers * capacity, TILE, arrived.shape[3])
    lists, counts = (
        lax.all_gather(box_tiles, "col", axis=0, tiled=True),
        lax.all_gather(box_count, "col", axis=0, tiled=True),
    )
    points = lax.all_gather(point_pos, "col", axis=1, tiled=True)
    partial_value = by_blocks(arrived, slot_alpha, slot_centre, lists, counts, points)
    density = lax.psum_scatter(
        partial_value.astype(jnp.bfloat16), "col", scatter_dimension=0, tiled=True
    ).astype(jnp.float32)
    return (rotated, density)


def solution(mesh):
    in_specs = (
        P(("row", "box"), "col"),
        P(("row", "box"), None),
        P(),
        P(),
        P(),
        P(),
        P(None, ("row", "col", "box"), None),
        P(),
        P(("row", "col", "box"), None),
        P(("row", "col", "box")),
    )
    out_specs = (P(("row", "box"), "col"), P(("row", "col", "box"), None))
    return jax.shard_map(
        per_device, mesh=mesh, in_specs=in_specs, out_specs=out_specs, check_vma=False
    )
```

profile of v0, /device:TPU:0, one launch (start us, length us, event | category | flops | bytes accessed | tf_op | source)
XLA Modules:
  0.0 196.5 jit_solution(6431484893824231304)
XLA Ops:
  7.2 5.5 %convolution_convert_fusion = bf16[256,128]{1,0:T(8,128)(2,1)} fusion(bf16[10240,256]{1,0:T(8,128)(2,1)} %param.13, bf16[10240,128]{1,0:T(8,128)(2,1)} %param.12), kind=kOutput, calls=%fused_computation.42 | convolution fusion | flops 671121408 | bytes 7929856 | tf_op jit(solution)/shard_map/dot_general | solution.py:61
  13.8 3.0 %copy.28 = bf16[10240,128]{0,1:T(8,128)(2,1)S(1)} copy(bf16[10240,128]{1,0:T(8,128)(2,1)} %param.12) | data formatting | bytes 5242880 | tf_op args[0]
  16.8 2.6 %copy.31 = f32[3,8192]{0,1:T(8,128)} copy(f32[3,8192]{1,0:T(4,128)S(1)} %copy-done.5) | data formatting | bytes 196608 | tf_op args[5]
  19.4 48.7 %all-reduce.4.cloned.1.call-done = bf16[256,128]{1,0:T(8,128)(2,1)} async-done(((bf16[256,128]{1,0:T(8,128)(2,1)}), bf16[256,128]{1,0:T(8,128)(2,1)}) %all-reduce.4.cloned.1.call-update) | async-done | bytes 65552 | tf_op jit(solution)/shard_map/psum | solution.py:62
  69.3 5.8 %fusion.13 = bf16[10240,128]{0,1:T(8,128)(2,1)} fusion(bf16[128,256]{1,0:T(8,128)(2,1)S(1)} %convolution_convert_fusion.1, bf16[10240,256]{1,0:T(8,128)(2,1)} %param.13, bf16[10240,128]{0,1:T(8,128)(2,1)S(1)} %copy.28), kind=kOutput, calls=%fused_computation.41 | convolution fusion | flops 675020800 | bytes 10551296 | tf_op jit(solution)/shard_map/dot_general | solution.py:65
  75.1 3.2 %copy.36 = bf16[10240,128]{1,0:T(8,128)(2,1)S(1)} copy(bf16[10240,128]{0,1:T(8,128)(2,1)} %fusion.13) | data formatting | bytes 5242880
  78.3 1.6 gather_fusion.7
  80.0 3.5 %all-to-all-start = ((bf16[8,2,128,128]{3,2,1,0:T(8,128)(2,1)}), bf16[8,2,128,128]{3,2,1,0:T(8,128)(2,1)S(1)}, u32[]{:S(2)}, u32[]{:S(2)}) async-start(bf16[8,2,128,128]{3,2,1,0:T(8,128)(2,1)} %bitcast.116), calls=%async_computation | async-start | bytes 1048576 | tf_op jit(solution)/shard_map/all_to_all | solution.py:80
  83.6 11.8 %gather_fusion.5 = s32[2048]{0:T(1024)S(1)} fusion(s32[81920]{0:T(1024)S(1)} %copy-done, s32[2048]{0:T(1024)S(1)} %fusion.15), kind=kCustom, calls=%fused_computation.5 | custom fusion | bytes 24576 | tf_op jit(solution)/shard_map/gather | solution.py:77
  95.4 7.7 %gather_fusion.6 = f32[2048,3]{1,0:T(8,128)S(1)} fusion(f32[3,8192]{0,1:T(8,128)} %copy.31, s32[2048]{0:T(1024)S(1)} %fusion.17), kind=kCustom, calls=%fused_computation.6 | custom fusion | bytes 57344 | tf_op jit(solution)/shard_map/gather | solution.py:77
  103.4 11.8 %gather_fusion.4 = f32[2048]{0:T(1024)S(1)} fusion(f32[81920]{0:T(1024)S(1)} %copy-done.1, s32[2048]{0:T(1024)S(1)} %fusion.15), kind=kCustom, calls=%fused_computation.4 | custom fusion | bytes 24576 | tf_op jit(solution)/shard_map/gather | solution.py:76
  116.8 8.3 %all-reduce = s32[16]{0:T(128)S(1)} all-reduce(s32[16]{0:T(128)S(1)} %dynamic-update-slice), channel_id=1, replica_groups=mesh['row'=2,'col'=4,'box'=4] {'col'}, use_global_device_ids=true, to_apply=%add | all-reduce | flops 16 | bytes 128
  125.1 13.1 %all_gather.11 = f32[3,16,128]{2,0,1:T(4,128)S(1)} all-gather(f32[3,4,128]{2,0,1:T(4,128)S(1)} %copy.29), channel_id=1, replica_groups=mesh['row'=2,'col'=4,'box'=4] {'col'}, dimensions={1}, use_global_device_ids=true | all-gather | bytes 30720 | tf_op jit(solution)/shard_map/all_gather | solution.py:86
  138.9 11.9 %all-gather = s32[4,4,16]{2,1,0:T(4,128)S(1)} all-gather(s32[1,4,16]{2,1,0:T(4,128)S(1)} %bitcast.126), channel_id=1, replica_groups=mesh['row'=2,'col'=4,'box'=4] {'col'}, dimensions={0}, use_global_device_ids=true | all-gather | bytes 1280 | tf_op jit(solution)/shard_map/all_gather | solution.py:83
  150.8 29.7 %while.10 = (s32[]{:T(128)}, bf16[8,2,128]{2,1,0:T(2,128)(2,1)S(1)}, s32[8,2]{1,0:T(8,128)S(1)}, s32[8,2,16]{2,1,0:T(2,128)S(1)}, f32[16,128]{1,0:T(8,128)S(1)},...) while((s32[]{:T(128)}, ...), condition=%wide.region_3.4_spmd, body=%wide.region_1.3_spmd.sunk | while | flops 140055680 | bytes 3644613 | solution.py:45
  153.3 1.2 fusion.41
  157.0 1.2 fusion.41
  160.7 1.2 fusion.41
  164.4 1.2 fusion.41
  168.1 1.2 fusion.41
  171.8 1.2 fusion.41
  175.5 1.2 fusion.41
  179.3 1.2 fusion.41
  180.5 8.6 %all-reduce.1 = bf16[16,128]{1,0:T(8,128)(2,1)S(1)} all-reduce(bf16[16,128]{1,0:T(8,128)(2,1)S(1)} %bitcast.125), channel_id=2, replica_groups=mesh['row'=2,'col'=4,'box'=4] {'col'}, use_global_device_ids=true, to_apply=%region_4.5.clone | all-reduce | flops 2048 | bytes 8192
  (186 shorter events, 23.4 us)
Async XLA Ops:
  7.2 76.4 %copy-start = (s32[81920]{0:T(1024)S(1)}, s32[81920]{0:T(1024)}, u32[]{:S(2)}) copy-start(s32[81920]{0:T(1024)} %param.16) | copy-start | bytes 983044
  7.2 5.7 %copy-start.2 = (s32[8,8,2]{1,2,0:T(2,128)S(1)}, s32[8,8,2]{1,2,0:T(2,128)}, u32[]{:S(2)}) copy-start(s32[8,8,2]{1,2,0:T(2,128)} %param.19) | copy-start | bytes 1540
  7.2 60.9 %all-reduce.4.cloned.1.call-start = ((), (), s32[]{:S(2)}) async-start(), calls=%async_computation.1 | async-start | bytes 131072 | tf_op jit(solution)/shard_map/psum | solution.py:62
  13.7 3.1 %copy-start.5 = (f32[3,8192]{1,0:T(4,128)S(1)}, f32[3,8192]{1,0:T(4,128)}, u32[]{:S(2)}) copy-start(f32[3,8192]{1,0:T(4,128)} %param.17) | copy-start | bytes 294916
  16.8 51.3 %copy-start.4 = (f32[256,256]{1,0:T(8,128)S(1)}, f32[256,256]{1,0:T(8,128)}, u32[]{:S(2)}) copy-start(f32[256,256]{1,0:T(8,128)} %param.14) | copy-start | bytes 786436
  78.3 5.2 %copy-start.3 = (bf16[10240,128]{1,0:T(8,128)(2,1)}, bf16[10240,128]{1,0:T(8,128)(2,1)S(1)}, u32[]{:S(2)}) copy-start(bf16[10240,128]{1,0:T(8,128)(2,1)S(1)} %copy.36) | copy-start | bytes 7864324
  80.0 70.8 %all-to-all-start = ((bf16[8,2,128,128]{3,2,1,0:T(8,128)(2,1)}), bf16[8,2,128,128]{3,2,1,0:T(8,128)(2,1)S(1)}, u32[]{:S(2)}, u32[]{:S(2)}) async-start(bf16[8,2,128,128]{3,2,1,0:T(8,128)(2,1)} %bitcast.116), calls=%async_computation | async-start | bytes 1048576 | tf_op jit(solution)/shard_map/all_to_all | solution.py:80
  95.4 8.1 %copy-start.1 = (f32[81920]{0:T(1024)S(1)}, f32[81920]{0:T(1024)}, u32[]{:S(2)}) copy-start(f32[81920]{0:T(1024)} %param.15) | copy-start | bytes 983044
  103.4 11.8 %copy-start.8 = (u32[32]{0:T(128)S(1)}, u32[32]{0:T(128)}, u32[]{:S(2)}) copy-start(u32[32]{0:T(128)} %constant.107) | copy-start | bytes 388
  103.4 13.1 %copy-start.9 = (s32[4]{0:T(128)S(1)}, s32[4]{0:T(128)}, u32[]{:S(2)}) copy-start(s32[4]{0:T(128)} %param.21) | copy-start | bytes 52
  103.4 21.7 %copy-start.6 = (f32[3,4,128]{2,1,0:T(4,128)S(1)}, f32[3,4,128]{2,1,0:T(4,128)}, u32[]{:S(2)}) copy-start(f32[3,4,128]{2,1,0:T(4,128)} %param.18) | copy-start | bytes 18436
  103.4 35.5 %copy-start.7 = (s32[4,16]{1,0:T(4,128)S(1)}, s32[4,16]{1,0:T(4,128)}, u32[]{:S(2)}) copy-start(s32[4,16]{1,0:T(4,128)} %param.20) | copy-start | bytes 772
Sparse Core Ops, SparseCore 0:
  12.9 55.1 all-reduce.3
where the time goes:
time: 197 us
  local copies, waits for them, and re-layouts  62.4 us (32%)
  waiting for transfers between devices  48.7 us (25%)
  blocking collectives  41.9 us (21%)
  matrix products  22.2 us (11%)
  between operations  15.6 us (8%)
  starting transfers between devices  3.53 us (2%)
    psum x1, waiting for transfers between devices, per_device(): lax.psum(panel_part.astype(jnp.bfloat16), ('row', 'box'))  48.7 us
    gather x3, local copies, waits for them, and re-layouts, per_device(): slot_centre = atom_pos[:, func_atom[funcs]]  19.8 us
    unnamed x2, blocking collectives  16.9 us
    all_gather x1, blocking collectives, per_device(): points = lax.all_gather(point_pos, 'col', axis=1, tiled=True)  13.1 us
    all_gather x1, blocking collectives, per_device(): lax.all_gather(box_tiles, 'col', axis=0, tiled=True)  11.9 us
    gather x1, local copies, waits for them, and re-layouts, per_device(): slot_alpha = func_exp[funcs]  11.8 us
    unnamed x27, local copies, waits for them, and re-layouts  9.83 us
    dot_general x8, matrix products, box_density(): orbital = jnp.dot(phi, block, preferred_element_type=jnp.float32)  9.66 us
  transfers between devices with their start and end apart: 2, of which 1 were waited for; matrix products, arithmetic and copies ran while one was open for 20% of the time, Pallas kernels for 0%

commit v1 on v0

--- a/solution.py
+++ b/solution.py
@@ -59,7 +59,7 @@
     box_count,
 ):
     panel_part = jnp.dot(reflectors.T, coeffs, preferred_element_type=jnp.float32)
-    panel = lax.psum(panel_part.astype(jnp.bfloat16), ("row", "box")).astype(jnp.float32)
+    panel = lax.psum(lax.psum(panel_part.astype(jnp.bfloat16), "box"), "row").astype(jnp.float32)
     scaled = jnp.dot(factor, panel, precision=lax.Precision.HIGHEST).astype(jnp.bfloat16)
     rotated = (
         coeffs.astype(jnp.float32) - jnp.dot(reflectors, scaled, preferred_element_type=jnp.float32)

time: 197 us -> 199 us (1.010)
    psum x1 -> x2, waiting for transfers between devices: 48.7 us -> 50.3 us  [the longest x1 27.2 us: per_device(): lax.psum(panel_part.astype(jnp.bfloat16), 'box')]
  transfers between devices with their start and end apart: 2 -> 3, of which waited for: 1 -> 2; matrix products, arithmetic and copies ran while one was open for 20% -> 20% of each run, Pallas kernels for 0% -> 0%
where the time goes in v1:
time: 199 us; the launch traced here: 198 us
  local copies, waits for them, and re-layouts  62.4 us (31%)
  waiting for transfers between devices  50.4 us (25%)
  blocking collectives  41.9 us (21%)
  matrix products  22.2 us (11%)
  between operations  15.6 us (8%)
  starting transfers between devices  3.57 us (2%)
    psum x1, waiting for transfers between devices, per_device(): lax.psum(panel_part.astype(jnp.bfloat16), 'box')  27.2 us
    psum x1, waiting for transfers between devices, per_device(): lax.psum(lax.psum(panel_part.astype(jnp.bfloat16), 'box'), 'row')  23.1 us
    gather x3, local copies, waits for them, and re-layouts, per_device(): slot_centre = atom_pos[:, func_atom[funcs]]  19.8 us
    unnamed x2, blocking collectives  16.9 us
    all_gather x1, blocking collectives, per_device(): points = lax.all_gather(point_pos, 'col', axis=1, tiled=True)  13.1 us
    all_gather x1, blocking collectives, per_device(): lax.all_gather(box_tiles, 'col', axis=0, tiled=True)  11.9 us
    gather x1, local copies, waits for them, and re-layouts, per_device(): slot_alpha = func_exp[funcs]  11.8 us
    unnamed x27, local copies, waits for them, and re-layouts  9.83 us
  transfers between devices with their start and end apart: 3, of which 2 were waited for; matrix products, arithmetic and copies ran while one was open for 20% of the time, Pallas kernels for 0%

profile of v1, /device:TPU:0, one launch (start us, length us, event | category | flops | bytes accessed | tf_op | source)
XLA Modules:
  0.0 198.2 jit_solution(6065969235184828179)
XLA Ops:
  7.2 5.5 %convolution_convert_fusion = bf16[256,128]{1,0:T(8,128)(2,1)} fusion(bf16[10240,256]{1,0:T(8,128)(2,1)} %param.13, bf16[10240,128]{1,0:T(8,128)(2,1)} %param.12), kind=kOutput, calls=%fused_computation.42 | convolution fusion | flops 671121408 | bytes 7929856 | tf_op jit(solution)/shard_map/dot_general | solution.py:61
  13.6 3.0 %copy.28 = bf16[10240,128]{0,1:T(8,128)(2,1)S(1)} copy(bf16[10240,128]{1,0:T(8,128)(2,1)} %param.12) | data formatting | bytes 5242880 | tf_op args[0]
  16.7 2.6 %copy.31 = f32[3,8192]{0,1:T(8,128)} copy(f32[3,8192]{1,0:T(4,128)S(1)} %copy-done.5) | data formatting | bytes 196608 | tf_op args[5]
  19.5 27.2 %all-reduce.5.cloned.1.call-done = bf16[256,128]{1,0:T(8,128)(2,1)} async-done(((bf16[256,128]{1,0:T(8,128)(2,1)}), bf16[256,128]{1,0:T(8,128)(2,1)}) %all-reduce.5.cloned.1.call-update) | async-done | bytes 65552 | tf_op jit(solution)/shard_map/psum | solution.py:62
  46.7 23.1 %all-reduce.7.cloned.1.call-done = bf16[256,128]{1,0:T(8,128)(2,1)} async-done(((bf16[256,128]{1,0:T(8,128)(2,1)}), bf16[256,128]{1,0:T(8,128)(2,1)}) %all-reduce.7.cloned.1.call-update) | async-done | bytes 65552 | tf_op jit(solution)/shard_map/psum | solution.py:62
  71.0 5.8 %fusion.13 = bf16[10240,128]{0,1:T(8,128)(2,1)} fusion(bf16[128,256]{1,0:T(8,128)(2,1)S(1)} %convolution_convert_fusion.1, bf16[10240,256]{1,0:T(8,128)(2,1)} %param.13, bf16[10240,128]{0,1:T(8,128)(2,1)S(1)} %copy.28), kind=kOutput, calls=%fused_computation.41 | convolution fusion | flops 675020800 | bytes 10551296 | tf_op jit(solution)/shard_map/dot_general | solution.py:65
  76.8 3.2 %copy.36 = bf16[10240,128]{1,0:T(8,128)(2,1)S(1)} copy(bf16[10240,128]{0,1:T(8,128)(2,1)} %fusion.13) | data formatting | bytes 5242880
  80.0 1.6 gather_fusion.7
  81.7 3.5 %all-to-all-start = ((bf16[8,2,128,128]{3,2,1,0:T(8,128)(2,1)}), bf16[8,2,128,128]{3,2,1,0:T(8,128)(2,1)S(1)}, u32[]{:S(2)}, u32[]{:S(2)}) async-start(bf16[8,2,128,128]{3,2,1,0:T(8,128)(2,1)} %bitcast.26), calls=%async_computation | async-start | bytes 1048576 | tf_op jit(solution)/shard_map/all_to_all | solution.py:80
  85.3 11.8 %gather_fusion.5 = s32[2048]{0:T(1024)S(1)} fusion(s32[81920]{0:T(1024)S(1)} %copy-done, s32[2048]{0:T(1024)S(1)} %fusion.15), kind=kCustom, calls=%fused_computation.5 | custom fusion | bytes 24576 | tf_op jit(solution)/shard_map/gather | solution.py:77
  97.1 7.7 %gather_fusion.6 = f32[2048,3]{1,0:T(8,128)S(1)} fusion(f32[3,8192]{0,1:T(8,128)} %copy.31, s32[2048]{0:T(1024)S(1)} %fusion.17), kind=kCustom, calls=%fused_computation.6 | custom fusion | bytes 57344 | tf_op jit(solution)/shard_map/gather | solution.py:77
  105.1 11.8 %gather_fusion.4 = f32[2048]{0:T(1024)S(1)} fusion(f32[81920]{0:T(1024)S(1)} %copy-done.1, s32[2048]{0:T(1024)S(1)} %fusion.15), kind=kCustom, calls=%fused_computation.4 | custom fusion | bytes 24576 | tf_op jit(solution)/shard_map/gather | solution.py:76
  118.5 8.3 %all-reduce = s32[16]{0:T(128)S(1)} all-reduce(s32[16]{0:T(128)S(1)} %dynamic-update-slice), channel_id=1, replica_groups=mesh['row'=2,'col'=4,'box'=4] {'col'}, use_global_device_ids=true, to_apply=%add | all-reduce | flops 16 | bytes 128
  126.8 13.1 %all_gather.11 = f32[3,16,128]{2,0,1:T(4,128)S(1)} all-gather(f32[3,4,128]{2,0,1:T(4,128)S(1)} %copy.29), channel_id=1, replica_groups=mesh['row'=2,'col'=4,'box'=4] {'col'}, dimensions={1}, use_global_device_ids=true | all-gather | bytes 30720 | tf_op jit(solution)/shard_map/all_gather | solution.py:86
  140.6 11.9 %all-gather = s32[4,4,16]{2,1,0:T(4,128)S(1)} all-gather(s32[1,4,16]{2,1,0:T(4,128)S(1)} %bitcast.125), channel_id=1, replica_groups=mesh['row'=2,'col'=4,'box'=4] {'col'}, dimensions={0}, use_global_device_ids=true | all-gather | bytes 1280 | tf_op jit(solution)/shard_map/all_gather | solution.py:83
  152.5 29.7 %while.10 = (s32[]{:T(128)}, bf16[8,2,128]{2,1,0:T(2,128)(2,1)S(1)}, s32[8,2]{1,0:T(8,128)S(1)}, s32[8,2,16]{2,1,0:T(2,128)S(1)}, f32[16,128]{1,0:T(8,128)S(1)},...) while((s32[]{:T(128)}, ...), condition=%wide.region_4.5_spmd, body=%wide.region_2.4_spmd.sunk | while | flops 140055680 | bytes 3644613 | solution.py:45
  155.0 1.2 fusion.41
  158.7 1.2 fusion.41
  162.4 1.2 fusion.41
  166.1 1.2 fusion.41
  169.8 1.2 fusion.41
  173.5 1.2 fusion.41
  177.2 1.2 fusion.41
  182.2 8.6 %all-reduce.1 = bf16[16,128]{1,0:T(8,128)(2,1)S(1)} all-reduce(bf16[16,128]{1,0:T(8,128)(2,1)S(1)} %bitcast.124), channel_id=2, replica_groups=mesh['row'=2,'col'=4,'box'=4] {'col'}, use_global_device_ids=true, to_apply=%region_5.6.clone | all-reduce | flops 2048 | bytes 8192
  (189 shorter events, 24.7 us)
Async XLA Ops:
  7.2 78.1 %copy-start = (s32[81920]{0:T(1024)S(1)}, s32[81920]{0:T(1024)}, u32[]{:S(2)}) copy-start(s32[81920]{0:T(1024)} %param.16) | copy-start | bytes 983044
  7.2 5.7 %copy-start.2 = (s32[8,8,2]{1,2,0:T(2,128)S(1)}, s32[8,8,2]{1,2,0:T(2,128)}, u32[]{:S(2)}) copy-start(s32[8,8,2]{1,2,0:T(2,128)} %param.19) | copy-start | bytes 1540
  7.2 39.5 %all-reduce.5.cloned.1.call-start = ((), (), s32[]{:S(2)}) async-start(), calls=%async_computation.1 | async-start | bytes 131072 | tf_op jit(solution)/shard_map/psum | solution.py:62
  12.8 57.0 %all-reduce.7.cloned.1.call-start = ((), (), s32[]{:S(2)}) async-start(), calls=%async_computation.2 | async-start | bytes 131072 | tf_op jit(solution)/shard_map/psum | solution.py:62
  13.6 3.1 %copy-start.5 = (f32[3,8192]{1,0:T(4,128)S(1)}, f32[3,8192]{1,0:T(4,128)}, u32[]{:S(2)}) copy-start(f32[3,8192]{1,0:T(4,128)} %param.17) | copy-start | bytes 294916
  16.6 53.2 %copy-start.4 = (f32[256,256]{1,0:T(8,128)S(1)}, f32[256,256]{1,0:T(8,128)}, u32[]{:S(2)}) copy-start(f32[256,256]{1,0:T(8,128)} %param.14) | copy-start | bytes 786436
  80.0 1.7 copy-start.3
  81.7 70.8 %all-to-all-start = ((bf16[8,2,128,128]{3,2,1,0:T(8,128)(2,1)}), bf16[8,2,128,128]{3,2,1,0:T(8,128)(2,1)S(1)}, u32[]{:S(2)}, u32[]{:S(2)}) async-start(bf16[8,2,128,128]{3,2,1,0:T(8,128)(2,1)} %bitcast.26), calls=%async_computation | async-start | bytes 1048576 | tf_op jit(solution)/shard_map/all_to_all | solution.py:80
  97.1 8.1 %copy-start.1 = (f32[81920]{0:T(1024)S(1)}, f32[81920]{0:T(1024)}, u32[]{:S(2)}) copy-start(f32[81920]{0:T(1024)} %param.15) | copy-start | bytes 983044
  105.1 11.8 %copy-start.8 = (u32[32]{0:T(128)S(1)}, u32[32]{0:T(128)}, u32[]{:S(2)}) copy-start(u32[32]{0:T(128)} %constant.107) | copy-start | bytes 388
  105.1 13.1 %copy-start.9 = (s32[4]{0:T(128)S(1)}, s32[4]{0:T(128)}, u32[]{:S(2)}) copy-start(s32[4]{0:T(128)} %param.21) | copy-start | bytes 52
  105.1 21.7 %copy-start.6 = (f32[3,4,128]{2,1,0:T(4,128)S(1)}, f32[3,4,128]{2,1,0:T(4,128)}, u32[]{:S(2)}) copy-start(f32[3,4,128]{2,1,0:T(4,128)} %param.18) | copy-start | bytes 18436
  105.1 35.5 %copy-start.7 = (s32[4,16]{1,0:T(4,128)S(1)}, s32[4,16]{1,0:T(4,128)}, u32[]{:S(2)}) copy-start(s32[4,16]{1,0:T(4,128)} %param.20) | copy-start | bytes 772
Sparse Core Ops, SparseCore 0:
  12.9 33.7 all-reduce.4
  49.0 20.7 all-reduce.6
